TPU v7x, 512 devices: a whole 4x8x8 slice. The times are simulated.
512 devices in a mesh: dp: 16 (over y, core), ctx: 32 (over z, x).
Axes of the slice: x: 4, y: 8, z: 8, core: 2. Of those that a mesh axis runs over, the one named last changes fastest.
Arguments:
- queries: bfloat16 [16, 4096, 4096], P('dp', 'ctx'), may hold values from -9 to 9
- keys: bfloat16 [16, 4096, 1024], P('dp', 'ctx'), may hold values from -9 to 9
- values: bfloat16 [16, 4096, 1024], P('dp', 'ctx'), may hold values from -6 to 6
- doc_lengths: int32 [16, 128], P('dp'), may hold values from 1 to 128, as said below
- cotangent: float32 [16, 128, 4096], P('dp', 'ctx'), may hold values from -50 to 50
- query_gain: float32 [128], replicated, may hold values from 0.6 to 4.5
- key_gain: float32 [128], replicated, may hold values from 0.6 to 4.5
Outputs:
- embed_quarter: float32 [16, 128, 1024], P('dp', 'ctx')
- embed_half: float32 [16, 128, 2048], P('dp', 'ctx')
- embed_full: float32 [16, 128, 4096], P('dp', 'ctx')
- grad_queries: bfloat16 [16, 4096, 4096], P('dp', 'ctx')
- grad_keys: bfloat16 [16, 4096, 1024], P('dp', 'ctx')
- grad_values: bfloat16 [16, 4096, 1024], P('dp', 'ctx')
- grad_query_gain: float32 [128], replicated
- grad_key_gain: float32 [128], replicated
Inputs may be any that keep to these rules, and one draw needn't show every extreme that they name: `doc_lengths`: each sequence's 128 lengths sum to 4096; the first of them is exactly 128. The last 65 documents of each sequence together span at most 128 tokens.
All inputs are finite; a program needn't handle non-finite values.
Results may differ from a plain program's by a relative error of at most 0.0054.
The roundings to bfloat16 on the way count: a program that leaves them out, or rounds other values in their place, can miss the bound.
Values may be sent and summed in bfloat16 or wider, within the bound.
A program may use at most 64 MiB of HBM per device.

v0:
```python
import math
import jax
import jax.numpy as jnp
from jax import lax
from jax.sharding import PartitionSpec as P

EPS = 1e-06


def rms_forward(field, gain):
    inverse = lax.rsqrt(jnp.mean(field * field, axis=-1, keepdims=True) + EPS)
    unit = field * inverse
    return (unit * gain, unit, inverse)


def rms_backward(grad, unit, inverse, gain):
    scaled = grad * gain
    inner = jnp.mean(scaled * unit, axis=-1, keepdims=True)
    grad_in = inverse * (scaled - unit * inner)
    grad_gain = jnp.sum((grad * unit).reshape(-1, unit.shape[-1]), axis=0)
    return (grad_in, grad_gain)


def doc_ids(lengths, positions, total):
    ends = jnp.cumsum(lengths, dtype=jnp.int32)
    owner = jnp.sum((positions[:, None] >= ends[None, :]).astype(jnp.int32), axis=1)
    inside = (positions >= 0) & (positions < total)
    return jnp.where(inside, owner, -1)


def block_probs(queries, keys, query_ids, key_ids):
    rows, heads, width = queries.shape
    query_groups = keys.shape[1]
    grouped = queries.reshape(rows, query_groups, heads // query_groups, width)
    scores = jnp.einsum("rgpe,kge->gprk", grouped, keys, preferred_element_type=jnp.float32) * (
        1.0 / math.sqrt(width)
    )
    allowed = query_ids[:, None] == key_ids[None, :]
    scores = jnp.where(allowed[None, None], scores, -jnp.inf)
    top = jnp.max(scores, axis=-1, keepdims=True)
    powers = jnp.exp(scores - top)
    return (powers / jnp.sum(powers, axis=-1, keepdims=True), grouped)


def forward_block(queries, keys, values, query_ids, key_ids):
    probs, grouped = block_probs(queries, keys, query_ids, key_ids)
    low = probs.astype(jnp.bfloat16)
    mixed = jnp.einsum("gprk,kge->rgpe", low, values, preferred_element_type=jnp.float32)
    return mixed.reshape(queries.shape[0], -1).astype(jnp.bfloat16)


def backward_block(queries, keys, values, query_ids, key_ids, grad_out):
    probs, grouped = block_probs(queries, keys, query_ids, key_ids)
    low = probs.astype(jnp.bfloat16)
    rows, heads, width = queries.shape
    query_groups = keys.shape[1]
    grad_four = grad_out.reshape(rows, query_groups, heads // query_groups, width)
    grad_probs = jnp.einsum("rgpe,kge->gprk", grad_four, values, preferred_element_type=jnp.float32)
    inner = jnp.sum(probs * grad_probs, axis=-1, keepdims=True)
    grad_scores = (probs * (grad_probs - inner)).astype(jnp.bfloat16)
    scale = 1.0 / math.sqrt(width)
    grad_q = (
        jnp.einsum("gprk,kge->rgpe", grad_scores, keys, preferred_element_type=jnp.float32) * scale
    )
    grad_k = (
        jnp.einsum("gprk,rgpe->kge", grad_scores, grouped, preferred_element_type=jnp.float32)
        * scale
    )
    grad_v = jnp.einsum("gprk,rgpe->kge", low, grad_four, preferred_element_type=jnp.float32)
    return (grad_q.reshape(rows, heads, width), grad_k, grad_v)


def band_setup(keys, values, lengths, margin, total):
    key_pad = jnp.pad(keys, ((margin, margin), (0, 0), (0, 0)))
    value_pad = jnp.pad(values, ((margin, margin), (0, 0), (0, 0)))
    pad_ids = doc_ids(lengths, jnp.arange(total + 2 * margin, dtype=jnp.int32) - margin, total)
    return (key_pad, value_pad, pad_ids)


def band_forward(normed, padded, token_ids, margin):
    key_pad, value_pad, pad_ids = padded
    total = normed.shape[0]
    block = min(512, 4 * margin)
    window = block + 2 * margin

    def forward(index):
        start = index * block
        return forward_block(
            lax.dynamic_slice_in_dim(normed, start, block, 0),
            lax.dynamic_slice_in_dim(key_pad, start, window, 0),
            lax.dynamic_slice_in_dim(value_pad, start, window, 0),
            lax.dynamic_slice_in_dim(token_ids, start, block, 0),
            lax.dynamic_slice_in_dim(pad_ids, start, window, 0),
        )

    return lax.map(forward, jnp.arange(total // block, dtype=jnp.int32)).reshape(total, -1)


def band_backward(normed, padded, token_ids, margin, grad_out):
    key_pad, value_pad, pad_ids = padded
    total, heads, width = normed.shape
    block = min(512, 4 * margin)
    window = block + 2 * margin
    zeros = jnp.zeros(key_pad.shape, jnp.float32)

    def backward(carry, index):
        key_acc, value_acc = carry
        start = index * block
        grad_q, grad_k, grad_v = backward_block(
            lax.dynamic_slice_in_dim(normed, start, block, 0),
            lax.dynamic_slice_in_dim(key_pad, start, window, 0),
            lax.dynamic_slice_in_dim(value_pad, start, window, 0),
            lax.dynamic_slice_in_dim(token_ids, start, block, 0),
            lax.dynamic_slice_in_dim(pad_ids, start, window, 0),
            lax.dynamic_slice_in_dim(grad_out, start, block, 0),
        )
        key_acc = lax.dynamic_update_slice_in_dim(
            key_acc, lax.dynamic_slice_in_dim(key_acc, start, window, 0) + grad_k, start, 0
        )
        value_acc = lax.dynamic_update_slice_in_dim(
            value_acc, lax.dynamic_slice_in_dim(value_acc, start, window, 0) + grad_v, start, 0
        )
        return ((key_acc, value_acc), grad_q)

    (key_acc, value_acc), grad_blocks = lax.scan(
        backward, (zeros, zeros), jnp.arange(total // block, dtype=jnp.int32)
    )
    return (
        grad_blocks.reshape(total, heads, width),
        key_acc[margin : margin + total],
        value_acc[margin : margin + total],
    )


def matryoshka(pooled, cotangent):
    width = pooled.shape[-1]
    prefixes = (width // 4, width // 2, width)

    def embed(field):
        return tuple(
            (
                field[:, :count]
                * lax.rsqrt(
                    jnp.sum(field[:, :count] * field[:, :count], axis=-1, keepdims=True) + EPS
                )
                for count in prefixes
            )
        )

    embeds, pullback = jax.vjp(embed, pooled)
    (grad,) = pullback(tuple((cotangent[:, :count] for count in prefixes)))
    return (embeds, grad)


def pool_tokens(attended, token_ids, docs, own_lengths):
    onehot = (token_ids[:, None] == jnp.arange(docs, dtype=jnp.int32)[None, :]).astype(jnp.bfloat16)
    partial_sums = jnp.dot(onehot.T, attended, preferred_element_type=jnp.float32)
    return lax.psum_scatter(partial_sums, "ctx", scatter_dimension=0, tiled=True) / own_lengths


def spread_tokens(scaled, token_ids):
    whole = lax.all_gather(scaled.astype(jnp.bfloat16), "ctx", axis=0, tiled=True).astype(
        scaled.dtype
    )
    return jnp.take(whole, token_ids, axis=0).astype(jnp.bfloat16)


def body(queries, keys, values, doc_lengths, cotangent, query_gain, key_gain):
    rows = queries.shape[1]
    model = queries.shape[2]
    width = query_gain.shape[0]
    heads = model // width
    kv_width = keys.shape[2]
    query_groups = kv_width // width
    group_repeat = heads // query_groups
    shards = lax.axis_size("ctx")
    position = lax.axis_index("ctx")
    total = rows * shards
    lengths = doc_lengths[0]
    docs = lengths.shape[0]
    owned = docs // shards
    own_ids = doc_ids(lengths, position * rows + jnp.arange(rows, dtype=jnp.int32), total)
    own_lengths = lax.dynamic_slice_in_dim(lengths, position * owned, owned).astype(jnp.float32)[
        :, None
    ]
    normed_kf, unit_k, inv_k = rms_forward(
        keys[0].astype(jnp.float32).reshape(rows, query_groups, width), key_gain
    )
    normed_k = normed_kf.astype(jnp.bfloat16)
    key_rep = jnp.repeat(normed_k, group_repeat, axis=1).reshape(rows, model)
    value_rep = jnp.repeat(
        values[0].reshape(rows, query_groups, width), group_repeat, axis=1
    ).reshape(rows, model)
    head_q, head_k, head_v = (
        lax.all_to_all(queries[0], "ctx", split_axis=1, concat_axis=0, tiled=True),
        lax.all_to_all(key_rep, "ctx", split_axis=1, concat_axis=0, tiled=True),
        lax.all_to_all(value_rep, "ctx", split_axis=1, concat_axis=0, tiled=True),
    )
    local_heads = model // shards // width
    normed_qf, unit_q, inv_q = rms_forward(
        head_q.astype(jnp.float32).reshape(total, local_heads, width), query_gain
    )
    normed_q = normed_qf.astype(jnp.bfloat16)
    all_ids = doc_ids(lengths, jnp.arange(total, dtype=jnp.int32), total)
    padded = band_setup(
        head_k.reshape(total, local_heads, width),
        head_v.reshape(total, local_heads, width),
        lengths,
        rows,
        total,
    )
    attended = band_forward(normed_q, padded, all_ids, rows)
    back_rows = lax.all_to_all(attended, "ctx", split_axis=0, concat_axis=1, tiled=True)
    pooled = pool_tokens(back_rows, own_ids, docs, own_lengths)
    embeds, grad_pooled = matryoshka(pooled, cotangent[0])
    grad_rows = spread_tokens(grad_pooled / own_lengths, own_ids)
    grad_out = lax.all_to_all(grad_rows, "ctx", split_axis=1, concat_axis=0, tiled=True)
    grad_nq, grad_head_k, grad_head_v = band_backward(normed_q, padded, all_ids, rows, grad_out)
    grad_qf, grad_qgain = rms_backward(grad_nq, unit_q, inv_q, query_gain)
    grad_q = lax.all_to_all(
        grad_qf.astype(jnp.bfloat16).reshape(total, local_heads * width),
        "ctx",
        split_axis=0,
        concat_axis=1,
        tiled=True,
    )
    share_k, share_v = (
        lax.all_to_all(
            grad_head_k.reshape(total, local_heads * width),
            "ctx",
            split_axis=0,
            concat_axis=1,
            tiled=True,
        ),
        lax.all_to_all(
            grad_head_v.reshape(total, local_heads * width),
            "ctx",
            split_axis=0,
            concat_axis=1,
            tiled=True,
        ),
    )
    grad_nk = jnp.sum(share_k.reshape(rows, query_groups, group_repeat, width), axis=2)
    grad_vf = jnp.sum(share_v.reshape(rows, query_groups, group_repeat, width), axis=2)
    grad_kf, grad_kgain = rms_backward(grad_nk, unit_k, inv_k, key_gain)
    total_qgain, total_kgain = lax.psum((grad_qgain, grad_kgain), ("dp", "ctx"))
    return (
        embeds[0][None],
        embeds[1][None],
        embeds[2][None],
        grad_q[None],
        grad_kf.astype(jnp.bfloat16).reshape(rows, kv_width)[None],
        grad_vf.astype(jnp.bfloat16).reshape(rows, kv_width)[None],
        total_qgain,
        total_kgain,
    )


def solution(mesh):
    in_specs = (
        P("dp", "ctx", None),
        P("dp", "ctx", None),
        P("dp", "ctx", None),
        P("dp", None),
        P("dp", "ctx", None),
        P(),
        P(),
    )
    out_specs = (
        P("dp", "ctx", None),
        P("dp", "ctx", None),
        P("dp", "ctx", None),
        P("dp", "ctx", None),
        P("dp", "ctx", None),
        P("dp", "ctx", None),
        P(),
        P(),
    )
    return jax.shard_map(body, mesh=mesh, in_specs=in_specs, out_specs=out_specs, check_vma=False)
```

profile of v0, /device:TPU:1, one launch (start us, length us, event | category | flops | bytes accessed | tf_op | source)
XLA Modules:
  0.0 838.3 jit_solution(9058164657707362389)
XLA Ops:
  9.4 13.7 %all-to-all-start = ((bf16[128,32,128]{2,0,1:T(8,128)(2,1)}), bf16[128,32,128]{2,0,1:T(8,128)(2,1)S(1)}, u32[]{:S(2)}, u32[]{:S(2)}) async-start(bf16[128,32,128]{2,0,1:T(8,128)(2,1)} %bitcast.29), calls=%async_computation | async-start | bytes 2097152 | tf_op jit(solution)/shard_map/all_to_all | solution.py:197
  24.8 24.6 %all-to-all-done = bf16[128,32,128]{2,0,1:T(8,128)(2,1)S(1)} async-done(((bf16[128,32,128]{2,0,1:T(8,128)(2,1)}), bf16[128,32,128]{2,0,1:T(8,128)(2,1)S(1)}, u32[]{:S(2)}, u32[]{:S(2)}) %all-to-all-start) | async-done | bytes 1048608 | tf_op jit(solution)/shard_map/all_to_all | solution.py:197
  50.6 6.4 all-to-all-start.1
  57.0 2.3 copy.106
  59.3 23.0 %all-to-all-done.1 = bf16[128,32,128]{2,0,1:T(8,128)(2,1)S(1)} async-done(((bf16[128,32,128]{2,0,1:T(8,128)(2,1)}), bf16[128,32,128]{2,0,1:T(8,128)(2,1)S(1)}, u32[]{:S(2)}, u32[]{:S(2)}) %all-to-all-start.1) | async-done | bytes 1048608 | tf_op jit(solution)/shard_map/all_to_all | solution.py:196
  82.2 6.8 all-to-all-start.2
  90.1 2.6 convert_reduce_fusion
  95.0 18.5 %all-to-all-done.2 = bf16[128,32,128]{0,2,1:T(8,128)(2,1)S(1)} async-done(((bf16[128,32,128]{0,2,1:T(8,128)(2,1)}), bf16[128,32,128]{0,2,1:T(8,128)(2,1)S(1)}, u32[]{:S(2)}, u32[]{:S(2)}) %all-to-all-start.2) | async-done | bytes 1048608 | tf_op jit(solution)/shard_map/all_to_all | solution.py:195
  113.5 1.7 convert_bitcast_fusion
  115.1 1.9 copy.107
  117.4 1.7 fusion.44
  119.0 41.8 %while.24 = (s32[]{:T(128)}, bf16[8,512,128]{2,1,0:T(8,128)(2,1)}, s32[8]{0:T(128)S(1)}, bf16[4352,1,128]{2,0,1:T(8,128)(2,1)}, s32[4096]{0:T(1024)S(1)}, /*inde...) while((s32[]{:T(128)}, bf16[8,512,128]{2,1,0:T(8,128)(2,1)}, ...), condition=%wide.region_9.10_spmd, body=%wide.region_6.9_spmd.sunk | while | flops 204930048 | bytes 5924080 | solution.py:96
  120.4 1.4 fusion.88
  130.9 1.4 fusion.88
  160.9 7.4 all-to-all-start.3
  168.5 24.6 %all-to-all-done.3 = bf16[32,128,128]{2,1,0:T(8,128)(2,1)S(1)} async-done(((bf16[32,128,128]{2,1,0:T(8,128)(2,1)}), bf16[32,128,128]{2,1,0:T(8,128)(2,1)S(1)}, u32[]{:S(2)}, u32[]{:S(2)}) %all-to-all-start.3) | async-done | bytes 1048608 | tf_op jit(solution)/shard_map/all_to_all | solution.py:213
  193.8 1.8 fusion.55
  197.7 160.3 %all-reduce.10.cloned.1.call-done = f32[128,4096]{1,0:T(8,128)} async-done(((f32[128,4096]{1,0:T(8,128)}), f32[128,4096]{1,0:T(8,128)}) %all-reduce.10.cloned.1.call-update) | async-done | bytes 2097168
  361.7 79.2 %all-gather.3.cloned.1.call-done = bf16[32,4,4096]{2,1,0:T(4,128)(2,1)} async-done(((bf16[1,4,4096]{2,1,0:T(4,128)(2,1)}), bf16[32,4,4096]{2,1,0:T(4,128)(2,1)}) %all-gather.3.cloned.1.call-update) | async-done | bytes 1048592 | tf_op jit(solution)/shard_map/all_gather | solution.py:162
  444.8 5.9 all-to-all-start.4
  451.4 21.0 %all-to-all-done.4 = bf16[128,32,128]{2,0,1:T(8,128)(2,1)} async-done(((bf16[128,32,128]{2,0,1:T(8,128)(2,1)}), bf16[128,32,128]{2,0,1:T(8,128)(2,1)}, u32[]{:S(2)}, u32[]{:S(2)}) %all-to-all-start.4) | async-done | bytes 1048608 | tf_op jit(solution)/shard_map/all_to_all | solution.py:217
  472.4 1.5 broadcast_in_dim.113.clone
  473.9 1.5 broadcast_in_dim.113.clone2
  475.4 106.8 %while.25 = (s32[]{:T(128)}, f32[4352,1,128]{2,0,1:T(8,128)}, f32[4352,1,128]{2,0,1:T(8,128)}, f32[8,512,1,128]{3,1,0,2:T(8,128)}, s32[8]{0:T(128)S(1)}, /*index...) while((s32[]{:T(128)}, f32[4352,1,128]{2,0,1:T(8,128)}, ...), condition=%wide.region_21.22_spmd, body=%wide.region_17.21_spmd.sunk | while | flops 510753280 | bytes 23696676 | solution.py:125
  482.4 1.4 fusion.100
  495.8 1.4 fusion.100
  509.1 1.4 fusion.100
  522.5 1.4 fusion.100
  535.8 1.4 fusion.100
  549.1 1.4 fusion.100
  562.5 1.4 fusion.100
  575.8 1.4 fusion.100
  582.2 3.1 copy.112
  585.3 3.1 multiply_reduce_fusion
  589.0 3.3 multiply_convert_fusion
  592.3 7.0 all-to-all-start.5
  599.4 1.5 slice.26
  600.8 2.9 copy.117
  603.8 17.2 %all-to-all-done.5 = bf16[32,128,128]{1,2,0:T(8,128)(2,1)S(1)} async-done(((bf16[32,128,128]{1,2,0:T(8,128)(2,1)}), bf16[32,128,128]{1,2,0:T(8,128)(2,1)S(1)}, u32[]{:S(2)}, u32[]{:S(2)}) %all-to-all-start.5) | async-done | bytes 1048608 | tf_op jit(solution)/shard_map/all_to_all | solution.py:220
  622.0 7.2 all-to-all-start.6
  629.2 3.1 slice.27
  632.3 2.9 copy.121
  635.2 38.2 %all-to-all-done.6 = f32[32,128,128]{1,2,0:T(8,128)S(1)} async-done(((f32[32,128,128]{1,2,0:T(8,128)}), f32[32,128,128]{1,2,0:T(8,128)S(1)}, u32[]{:S(2)}, u32[]{:S(2)}) %all-to-all-start.6) | async-done | bytes 2097184 | tf_op jit(solution)/shard_map/all_to_all | solution.py:228
  673.4 8.6 %all-to-all-start.7 = ((f32[32,128,128]{1,2,0:T(8,128)}), f32[32,128,128]{1,2,0:T(8,128)}, u32[]{:S(2)}, u32[]{:S(2)}) async-start(f32[32,128,128]{1,2,0:T(8,128)} %copy.121), calls=%async_computation.7 | async-start | bytes 4194304 | tf_op jit(solution)/shard_map/all_to_all | solution.py:235
  682.0 2.3 copy.125
  686.2 40.4 %all-to-all-done.7 = f32[32,128,128]{1,2,0:T(8,128)} async-done(((f32[32,128,128]{1,2,0:T(8,128)}), f32[32,128,128]{1,2,0:T(8,128)}, u32[]{:S(2)}, u32[]{:S(2)}) %all-to-all-start.7) | async-done | bytes 2097184 | tf_op jit(solution)/shard_map/all_to_all | solution.py:235
  726.6 1.8 bitcast_reduce_fusion
  729.5 102.0 %all-reduce.7 = (f32[128]{0:T(128)}, f32[128]{0:T(128)}) all-reduce(f32[128]{0:T(128)S(1)} %copy-done.19, f32[128]{0:T(128)S(1)} %bitcast_reduce_fusion.2), channel_id=1, replica_groups=mesh['dp'=16,'ctx'=32] {'dp','ctx'}, use_global_device_ids=true, to_apply=%region_27.28 | all-reduce | flops 256 | bytes 2048 | tf_op jit(solution)/shard_map/psum | solution.py:246
  (307 shorter events, 146.6 us)
Async XLA Ops:
  8.2 15.0 %copy-start.9 = (bf16[1,128,1024]{2,1,0:T(8,128)(2,1)S(1)}, bf16[1,128,1024]{2,1,0:T(8,128)(2,1)}, u32[]{:S(2)}) copy-start(bf16[1,128,1024]{2,1,0:T(8,128)(2,1)} %param.12) | copy-start | bytes 786436
  8.2 16.0 %copy-start.13 = (f32[128]{0:T(128)S(1)}, f32[128]{0:T(128)}, u32[]{:S(2)}) copy-start(f32[128]{0:T(128)} %param.17) | copy-start | bytes 1540
  9.4 39.9 %all-to-all-start = ((bf16[128,32,128]{2,0,1:T(8,128)(2,1)}), bf16[128,32,128]{2,0,1:T(8,128)(2,1)S(1)}, u32[]{:S(2)}, u32[]{:S(2)}) async-start(bf16[128,32,128]{2,0,1:T(8,128)(2,1)} %bitcast.29), calls=%async_computation | async-start | bytes 2097152 | tf_op jit(solution)/shard_map/all_to_all | solution.py:197
  23.4 0.8 copy-start.5
  23.4 27.1 %copy-start.10 = (f32[128,8]{0,1:T(8,128)}, f32[128,8]{0,1:T(8,128)S(1)}, u32[]{:S(2)}) copy-start(f32[128,8]{0,1:T(8,128)S(1)} %add_rsqrt_fusion.1) | copy-start | bytes 12292
  50.6 31.6 %all-to-all-start.1 = ((bf16[128,32,128]{2,0,1:T(8,128)(2,1)}), bf16[128,32,128]{2,0,1:T(8,128)(2,1)S(1)}, u32[]{:S(2)}, u32[]{:S(2)}) async-start(bf16[128,32,128]{2,0,1:T(8,128)(2,1)} %bitcast.33), calls=%async_computation.1 | async-start | bytes 2097152 | tf_op jit(solution)/shard_map/all_to_all | solution.py:196
  57.0 32.1 %copy-start.17 = (s32[1,128]{1,0:T(1,128)S(1)}, s32[1,128]{1,0:T(1,128)}, u32[]{:S(2)}) copy-start(s32[1,128]{1,0:T(1,128)} %param.14) | copy-start | bytes 1540
  82.2 31.2 %all-to-all-start.2 = ((bf16[128,32,128]{0,2,1:T(8,128)(2,1)}), bf16[128,32,128]{0,2,1:T(8,128)(2,1)S(1)}, u32[]{:S(2)}, u32[]{:S(2)}) async-start(bf16[128,32,128]{0,2,1:T(8,128)(2,1)} %bitcast.243), calls=%async_computation.2 | async-start | bytes 2097152 | tf_op jit(solution)/shard_map/all_to_all | solution.py:195
  113.5 3.6 copy-start.3
  115.1 2.2 copy-start.15
  117.1 2.0 copy-start
  160.9 32.3 %all-to-all-start.3 = ((bf16[32,128,128]{2,1,0:T(8,128)(2,1)}), bf16[32,128,128]{2,1,0:T(8,128)(2,1)S(1)}, u32[]{:S(2)}, u32[]{:S(2)}) async-start(bf16[32,128,128]{2,1,0:T(8,128)(2,1)} %bitcast.247), calls=%async_computation.3 | async-start | bytes 2097152 | tf_op jit(solution)/shard_map/all_to_all | solution.py:213
  168.3 189.7 %all-reduce.10.cloned.1.call-start = ((), (), s32[]{:S(2)}) async-start(), calls=%async_computation.9 | async-start | bytes 4194304
  193.8 3.9 copy-start.18
  193.8 164.2 %copy-start.8 = (f32[1,4,4096]{2,1,0:T(4,128)S(1)}, f32[1,4,4096]{2,1,0:T(4,128)}, u32[]{:S(2)}) copy-start(f32[1,4,4096]{2,1,0:T(4,128)} %param.15) | copy-start | bytes 196612
  195.6 245.3 %all-gather.3.cloned.1.call-start = ((), (), s32[]{:S(2)}) async-start(), calls=%async_computation.8 | async-start | bytes 1081344 | tf_op jit(solution)/shard_map/all_gather | solution.py:162
  444.8 27.6 %all-to-all-start.4 = ((bf16[128,32,128]{2,0,1:T(8,128)(2,1)}), bf16[128,32,128]{2,0,1:T(8,128)(2,1)}, u32[]{:S(2)}, u32[]{:S(2)}) async-start(bf16[128,32,128]{2,0,1:T(8,128)(2,1)} %fusion.42), calls=%async_computation.4 | async-start | bytes 2097152 | tf_op jit(solution)/shard_map/all_to_all | solution.py:217
  582.2 3.1 copy-start.1
  582.2 3.1 copy-start.12
  582.2 3.1 copy-start.16
  585.3 3.8 copy-start.4
  589.0 10.3 %copy-start.2 = (f32[4352,1,128]{2,0,1:T(8,128)S(1)}, f32[4352,1,128]{2,0,1:T(8,128)}, u32[]{:S(2)}) copy-start(f32[4352,1,128]{2,0,1:T(8,128)} %get-tuple-element.111) | copy-start | bytes 6684676
  592.3 28.6 %all-to-all-start.5 = ((bf16[32,128,128]{1,2,0:T(8,128)(2,1)}), bf16[32,128,128]{1,2,0:T(8,128)(2,1)S(1)}, u32[]{:S(2)}, u32[]{:S(2)}) async-start(bf16[32,128,128]{1,2,0:T(8,128)(2,1)} %multiply_convert_fusion), calls=%async_computation.5 | async-start | bytes 2097152 | tf_op jit(solution)/shard_map/all_to_all | solution.py:220
  621.0 1.0 copy-start.7
  622.0 51.4 %all-to-all-start.6 = ((f32[32,128,128]{1,2,0:T(8,128)}), f32[32,128,128]{1,2,0:T(8,128)S(1)}, u32[]{:S(2)}, u32[]{:S(2)}) async-start(f32[32,128,128]{1,2,0:T(8,128)} %copy.117), calls=%async_computation.6 | async-start | bytes 4194304 | tf_op jit(solution)/shard_map/all_to_all | solution.py:228
  635.1 46.8 %copy-start.14 = (f32[128]{0:T(128)S(1)}, f32[128]{0:T(128)}, u32[]{:S(2)}) copy-start(f32[128]{0:T(128)} %param.17) | copy-start | bytes 1540
  673.4 53.3 %all-to-all-start.7 = ((f32[32,128,128]{1,2,0:T(8,128)}), f32[32,128,128]{1,2,0:T(8,128)}, u32[]{:S(2)}, u32[]{:S(2)}) async-start(f32[32,128,128]{1,2,0:T(8,128)} %copy.121), calls=%async_computation.7 | async-start | bytes 4194304 | tf_op jit(solution)/shard_map/all_to_all | solution.py:235
  681.9 2.5 copy-start.6
  682.0 2.5 copy-start.11
  686.2 43.3 %copy-start.19 = (f32[128]{0:T(128)S(1)}, f32[128]{0:T(128)}, u32[]{:S(2)}) copy-start(f32[128]{0:T(128)} %get-tuple-element.153) | copy-start | bytes 1540
Sparse Core Ops, SparseCore 0:
  195.8 162.1 all-reduce.9
  362.2 78.6 all-gather.2
where the time goes:
time: 841 us; the launch traced here: 838 us
  waiting for transfers between devices  447 us (53%)
  blocking collectives  102 us (12%)
  local copies, waits for them, and re-layouts  92.7 us (11%)
  matrix products  77.2 us (9%)
  starting transfers between devices  63.1 us (8%)
  other arithmetic  29.8 us (4%)
  between operations  15.2 us (2%)
  loops' own time  11.5 us (1%)
    unnamed x3, waiting for transfers between devices  160 us
    psum x1, blocking collectives, body(): total_qgain, total_kgain = lax.psum((grad_qgain, grad_kgain), ('dp', 'ctx'))  102 us
    all_gather x1, waiting for transfers between devices, spread_tokens(): lax.all_gather(scaled.astype(jnp.bfloat16), 'ctx', axis=0, tiled=True)  79.2 us
    all_to_all x1, waiting for transfers between devices, body(): lax.all_to_all(grad_head_v.reshape(total, local_heads * width), 'ctx', sp...  40.4 us
    all_to_all x1, waiting for transfers between devices, body(): lax.all_to_all(grad_head_k.reshape(total, local_heads * width), 'ctx', sp...  38.2 us
    all_to_all x1, waiting for transfers between devices, body(): lax.all_to_all(value_rep, 'ctx', split_axis=1, concat_axis=0, tiled=True)  24.6 us
    all_to_all x1, waiting for transfers between devices, body(): lax.all_to_all(attended, 'ctx', split_axis=0, concat_axis=1, tiled=True)  24.6 us
    all_to_all x1, waiting for transfers between devices, body(): lax.all_to_all(key_rep, 'ctx', split_axis=1, concat_axis=0, tiled=True)  23 us
  transfers between devices with their start and end apart: 10, of which 10 were waited for; matrix products, arithmetic and copies ran while one was open for 3% of the time, Pallas kernels for 0%

commit v1 on v0

--- a/solution.py
+++ b/solution.py
@@ -5,6 +5,13 @@
 from jax.sharding import PartitionSpec as P
 
 EPS = 1e-06
+
+
+def exchange_gather(x, name, d):
+    devices = lax.axis_size(name)
+    blocks = jnp.stack([x for _ in range(devices)])
+    blocks = lax.all_to_all(blocks, name, split_axis=0, concat_axis=0)
+    return jnp.concatenate(blocks, axis=d)
 
 
 def rms_forward(field, gain):
@@ -159,9 +166,7 @@
 
 
 def spread_tokens(scaled, token_ids):
-    whole = lax.all_gather(scaled.astype(jnp.bfloat16), "ctx", axis=0, tiled=True).astype(
-        scaled.dtype
-    )
+    whole = exchange_gather(scaled.astype(jnp.bfloat16), "ctx", 0).astype(scaled.dtype)
     return jnp.take(whole, token_ids, axis=0).astype(jnp.bfloat16)
 
 

time: 841 us -> 800 us (0.951)
  waiting for transfers between devices: 447 us -> 392 us
  starting transfers between devices: 63.1 us -> 71.8 us
    all_gather x1 -> x0, waiting for transfers between devices: 79.2 us -> none  [spread_tokens(): lax.all_gather(scaled.astype(jnp.bfloat16), 'ctx', axis=0, tiled=True)]
    all_to_all x0 -> x1, waiting for transfers between devices: none -> 21.8 us  [exchange_gather(): blocks = lax.all_to_all(blocks, name, split_axis=0, concat_axis=0)]
    unnamed x3 -> x2, waiting for transfers between devices: 160 us -> 160 us
where the time goes in v1:
time: 800 us; the launch traced here: 797 us
  waiting for transfers between devices  392 us (49%)
  blocking collectives  101 us (13%)
  local copies, waits for them, and re-layouts  98.5 us (12%)
  matrix products  77.2 us (10%)
  starting transfers between devices  71.8 us (9%)
  other arithmetic  29.8 us (4%)
  between operations  15.2 us (2%)
  loops' own time  11.5 us (1%)
    unnamed x2, waiting for transfers between devices  160 us
    psum x1, blocking collectives, body(): total_qgain, total_kgain = lax.psum((grad_qgain, grad_kgain), ('dp', 'ctx'))  101 us
    all_to_all x1, waiting for transfers between devices, body(): lax.all_to_all(grad_head_v.reshape(total, local_heads * width), 'ctx', sp...  41.4 us
    all_to_all x1, waiting for transfers between devices, body(): lax.all_to_all(grad_head_k.reshape(total, local_heads * width), 'ctx', sp...  38.7 us
    all_to_all x1, waiting for transfers between devices, body(): lax.all_to_all(value_rep, 'ctx', split_axis=1, concat_axis=0, tiled=True)  24.6 us
    all_to_all x1, waiting for transfers between devices, body(): lax.all_to_all(attended, 'ctx', split_axis=0, concat_axis=1, tiled=True)  24.6 us
    all_to_all x1, waiting for transfers between devices, body(): lax.all_to_all(key_rep, 'ctx', split_axis=1, concat_axis=0, tiled=True)  23 us
    dot_general x16, matrix products, block_probs(): jnp.einsum('rgpe,kge->gprk', grouped, keys, preferred_element_type=jnp.fl...  22.2 us
  transfers between devices with their start and end apart: 10, of which 10 were waited for; matrix products, arithmetic and copies ran while one was open for 3% of the time, Pallas kernels for 0%

profile of v1, /device:TPU:1, one launch (start us, length us, event | category | flops | bytes accessed | tf_op | source)
XLA Modules:
  0.0 796.9 jit_solution(9833089151682916428)
XLA Ops:
  9.4 13.7 %all-to-all-start = ((bf16[128,32,128]{2,0,1:T(8,128)(2,1)}), bf16[128,32,128]{2,0,1:T(8,128)(2,1)S(1)}, u32[]{:S(2)}, u32[]{:S(2)}) async-start(bf16[128,32,128]{2,0,1:T(8,128)(2,1)} %bitcast.29), calls=%async_computation | async-start | bytes 2097152 | tf_op jit(solution)/shard_map/all_to_all | solution.py:202
  24.8 24.6 %all-to-all-done = bf16[128,32,128]{2,0,1:T(8,128)(2,1)S(1)} async-done(((bf16[128,32,128]{2,0,1:T(8,128)(2,1)}), bf16[128,32,128]{2,0,1:T(8,128)(2,1)S(1)}, u32[]{:S(2)}, u32[]{:S(2)}) %all-to-all-start) | async-done | bytes 1048608 | tf_op jit(solution)/shard_map/all_to_all | solution.py:202
  50.6 6.4 all-to-all-start.1
  57.0 2.3 copy.106
  59.3 23.0 %all-to-all-done.1 = bf16[128,32,128]{2,0,1:T(8,128)(2,1)S(1)} async-done(((bf16[128,32,128]{2,0,1:T(8,128)(2,1)}), bf16[128,32,128]{2,0,1:T(8,128)(2,1)S(1)}, u32[]{:S(2)}, u32[]{:S(2)}) %all-to-all-start.1) | async-done | bytes 1048608 | tf_op jit(solution)/shard_map/all_to_all | solution.py:201
  82.2 6.8 all-to-all-start.2
  90.1 2.6 convert_reduce_fusion
  95.0 18.5 %all-to-all-done.2 = bf16[128,32,128]{0,2,1:T(8,128)(2,1)S(1)} async-done(((bf16[128,32,128]{0,2,1:T(8,128)(2,1)}), bf16[128,32,128]{0,2,1:T(8,128)(2,1)S(1)}, u32[]{:S(2)}, u32[]{:S(2)}) %all-to-all-start.2) | async-done | bytes 1048608 | tf_op jit(solution)/shard_map/all_to_all | solution.py:200
  113.5 1.7 convert_bitcast_fusion
  115.1 1.9 copy.107
  117.4 1.7 fusion.44
  119.0 41.8 %while.24 = (s32[]{:T(128)}, bf16[8,512,128]{2,1,0:T(8,128)(2,1)}, s32[8]{0:T(128)S(1)}, bf16[4352,1,128]{2,0,1:T(8,128)(2,1)}, s32[4096]{0:T(1024)S(1)}, /*inde...) while((s32[]{:T(128)}, bf16[8,512,128]{2,1,0:T(8,128)(2,1)}, ...), condition=%wide.region_9.10_spmd, body=%wide.region_6.9_spmd.sunk | while | flops 204930048 | bytes 5924080 | solution.py:103
  160.8 7.4 all-to-all-start.3
  168.5 24.6 %all-to-all-done.3 = bf16[32,128,128]{2,1,0:T(8,128)(2,1)S(1)} async-done(((bf16[32,128,128]{2,1,0:T(8,128)(2,1)}), bf16[32,128,128]{2,1,0:T(8,128)(2,1)S(1)}, u32[]{:S(2)}, u32[]{:S(2)}) %all-to-all-start.3) | async-done | bytes 1048608 | tf_op jit(solution)/shard_map/all_to_all | solution.py:218
  193.8 1.8 fusion.55
  197.7 160.3 %all-reduce.10.cloned.1.call-done = f32[128,4096]{1,0:T(8,128)} async-done(((f32[128,4096]{1,0:T(8,128)}), f32[128,4096]{1,0:T(8,128)}) %all-reduce.10.cloned.1.call-update) | async-done | bytes 2097168
  361.6 1.4 stack.2
  363.1 5.5 all-to-all-start.4
  368.6 21.8 %all-to-all-done.4 = bf16[32,4,4096]{2,1,0:T(4,128)(2,1)S(1)} async-done(((bf16[32,4,4096]{2,1,0:T(4,128)(2,1)}), bf16[32,4,4096]{2,1,0:T(4,128)(2,1)S(1)}, u32[]{:S(2)}, u32[]{:S(2)}) %all-to-all-start.4) | async-done | bytes 1048608 | tf_op jit(solution)/shard_map/all_to_all | solution.py:13
  393.2 8.3 %all-to-all-start.5 = ((bf16[128,32,128]{2,0,1:T(8,128)(2,1)}), bf16[128,32,128]{2,0,1:T(8,128)(2,1)}, u32[]{:S(2)}, u32[]{:S(2)}) async-start(bf16[128,32,128]{2,0,1:T(8,128)(2,1)} %fusion.42), calls=%async_computation.5 | async-start | bytes 2097152 | tf_op jit(solution)/shard_map/all_to_all | solution.py:222
  402.1 21.4 %all-to-all-done.5 = bf16[128,32,128]{2,0,1:T(8,128)(2,1)} async-done(((bf16[128,32,128]{2,0,1:T(8,128)(2,1)}), bf16[128,32,128]{2,0,1:T(8,128)(2,1)}, u32[]{:S(2)}, u32[]{:S(2)}) %all-to-all-start.5) | async-done | bytes 1048608 | tf_op jit(solution)/shard_map/all_to_all | solution.py:222
  423.5 1.5 broadcast_in_dim.113.clone
  425.0 1.5 broadcast_in_dim.113.clone2
  426.6 112.2 %while.25 = (s32[]{:T(128)}, f32[4352,1,128]{2,0,1:T(8,128)}, f32[4352,1,128]{2,0,1:T(8,128)}, f32[8,512,1,128]{3,1,0,2:T(8,128)}, s32[8]{0:T(128)S(1)}, /*index...) while((s32[]{:T(128)}, f32[4352,1,128]{2,0,1:T(8,128)}, ...), condition=%wide.region_21.22_spmd, body=%wide.region_17.21_spmd.sunk | while | flops 510753280 | bytes 23696676 | solution.py:132
  434.2 1.4 fusion.99
  448.3 1.4 fusion.99
  462.3 1.4 fusion.99
  476.4 1.4 fusion.99
  490.4 1.4 fusion.99
  504.4 1.4 fusion.99
  518.4 1.4 fusion.99
  532.5 1.4 fusion.99
  538.8 3.1 copy.112
  541.9 3.1 multiply_reduce_fusion
  545.7 3.3 multiply_convert_fusion
  548.9 7.6 all-to-all-start.6
  556.6 1.5 slice.26
  558.1 2.9 copy.117
  561.0 17.7 %all-to-all-done.6 = bf16[32,128,128]{1,2,0:T(8,128)(2,1)S(1)} async-done(((bf16[32,128,128]{1,2,0:T(8,128)(2,1)}), bf16[32,128,128]{1,2,0:T(8,128)(2,1)S(1)}, u32[]{:S(2)}, u32[]{:S(2)}) %all-to-all-start.6) | async-done | bytes 1048608 | tf_op jit(solution)/shard_map/all_to_all | solution.py:225
  579.7 7.8 all-to-all-start.7
  587.5 3.1 slice.27
  590.6 2.9 copy.121
  593.5 38.7 %all-to-all-done.7 = f32[32,128,128]{1,2,0:T(8,128)S(1)} async-done(((f32[32,128,128]{1,2,0:T(8,128)}), f32[32,128,128]{1,2,0:T(8,128)S(1)}, u32[]{:S(2)}, u32[]{:S(2)}) %all-to-all-start.7) | async-done | bytes 2097184 | tf_op jit(solution)/shard_map/all_to_all | solution.py:233
  632.2 8.3 %all-to-all-start.8 = ((f32[32,128,128]{1,2,0:T(8,128)}), f32[32,128,128]{1,2,0:T(8,128)}, u32[]{:S(2)}, u32[]{:S(2)}) async-start(f32[32,128,128]{1,2,0:T(8,128)} %copy.121), calls=%async_computation.8 | async-start | bytes 4194304 | tf_op jit(solution)/shard_map/all_to_all | solution.py:240
  640.6 2.3 copy.125
  644.9 41.4 %all-to-all-done.8 = f32[32,128,128]{1,2,0:T(8,128)} async-done(((f32[32,128,128]{1,2,0:T(8,128)}), f32[32,128,128]{1,2,0:T(8,128)}, u32[]{:S(2)}, u32[]{:S(2)}) %all-to-all-start.8) | async-done | bytes 2097184 | tf_op jit(solution)/shard_map/all_to_all | solution.py:240
  686.3 1.8 bitcast_reduce_fusion
  689.2 100.9 %all-reduce.7 = (f32[128]{0:T(128)}, f32[128]{0:T(128)}) all-reduce(f32[128]{0:T(128)S(1)} %copy-done.20, f32[128]{0:T(128)S(1)} %bitcast_reduce_fusion.2), channel_id=1, replica_groups=mesh['dp'=16,'ctx'=32] {'dp','ctx'}, use_global_device_ids=true, to_apply=%region_27.28 | all-reduce | flops 256 | bytes 2048 | tf_op jit(solution)/shard_map/psum | solution.py:251
  (309 shorter events, 153.7 us)
Async XLA Ops:
  8.2 15.0 %copy-start.9 = (bf16[1,128,1024]{2,1,0:T(8,128)(2,1)S(1)}, bf16[1,128,1024]{2,1,0:T(8,128)(2,1)}, u32[]{:S(2)}) copy-start(bf16[1,128,1024]{2,1,0:T(8,128)(2,1)} %param.12) | copy-start | bytes 786436
  8.2 16.0 %copy-start.14 = (f32[128]{0:T(128)S(1)}, f32[128]{0:T(128)}, u32[]{:S(2)}) copy-start(f32[128]{0:T(128)} %param.17) | copy-start | bytes 1540
  9.4 39.9 %all-to-all-start = ((bf16[128,32,128]{2,0,1:T(8,128)(2,1)}), bf16[128,32,128]{2,0,1:T(8,128)(2,1)S(1)}, u32[]{:S(2)}, u32[]{:S(2)}) async-start(bf16[128,32,128]{2,0,1:T(8,128)(2,1)} %bitcast.29), calls=%async_computation | async-start | bytes 2097152 | tf_op jit(solution)/shard_map/all_to_all | solution.py:202
  23.4 0.8 copy-start.5
  23.4 27.1 %copy-start.11 = (f32[128,8]{0,1:T(8,128)}, f32[128,8]{0,1:T(8,128)S(1)}, u32[]{:S(2)}) copy-start(f32[128,8]{0,1:T(8,128)S(1)} %add_rsqrt_fusion.1) | copy-start | bytes 12292
  50.6 31.6 %all-to-all-start.1 = ((bf16[128,32,128]{2,0,1:T(8,128)(2,1)}), bf16[128,32,128]{2,0,1:T(8,128)(2,1)S(1)}, u32[]{:S(2)}, u32[]{:S(2)}) async-start(bf16[128,32,128]{2,0,1:T(8,128)(2,1)} %bitcast.33), calls=%async_computation.1 | async-start | bytes 2097152 | tf_op jit(solution)/shard_map/all_to_all | solution.py:201
  57.0 32.1 %copy-start.18 = (s32[1,128]{1,0:T(1,128)S(1)}, s32[1,128]{1,0:T(1,128)}, u32[]{:S(2)}) copy-start(s32[1,128]{1,0:T(1,128)} %param.14) | copy-start | bytes 1540
  82.2 31.2 %all-to-all-start.2 = ((bf16[128,32,128]{0,2,1:T(8,128)(2,1)}), bf16[128,32,128]{0,2,1:T(8,128)(2,1)S(1)}, u32[]{:S(2)}, u32[]{:S(2)}) async-start(bf16[128,32,128]{0,2,1:T(8,128)(2,1)} %bitcast.241), calls=%async_computation.2 | async-start | bytes 2097152 | tf_op jit(solution)/shard_map/all_to_all | solution.py:200
  113.5 3.6 copy-start.3
  115.1 2.2 copy-start.16
  117.1 2.0 copy-start
  160.8 32.9 %copy-start.10 = (s32[4096]{0:T(1024)}, s32[4096]{0:T(1024)S(1)}, u32[]{:S(2)}) copy-start(s32[4096]{0:T(1024)S(1)} %get-tuple-element.473) | copy-start | bytes 49156
  160.8 32.3 %all-to-all-start.3 = ((bf16[32,128,128]{2,1,0:T(8,128)(2,1)}), bf16[32,128,128]{2,1,0:T(8,128)(2,1)S(1)}, u32[]{:S(2)}, u32[]{:S(2)}) async-start(bf16[32,128,128]{2,1,0:T(8,128)(2,1)} %bitcast.245), calls=%async_computation.3 | async-start | bytes 2097152 | tf_op jit(solution)/shard_map/all_to_all | solution.py:218
  168.3 189.7 %all-reduce.10.cloned.1.call-start = ((), (), s32[]{:S(2)}) async-start(), calls=%async_computation.9 | async-start | bytes 4194304
  193.8 3.8 copy-start.19
  193.8 164.2 %copy-start.8 = (f32[1,4,4096]{2,1,0:T(4,128)S(1)}, f32[1,4,4096]{2,1,0:T(4,128)}, u32[]{:S(2)}) copy-start(f32[1,4,4096]{2,1,0:T(4,128)} %param.15) | copy-start | bytes 196612
  363.1 27.3 %all-to-all-start.4 = ((bf16[32,4,4096]{2,1,0:T(4,128)(2,1)}), bf16[32,4,4096]{2,1,0:T(4,128)(2,1)S(1)}, u32[]{:S(2)}, u32[]{:S(2)}) async-start(bf16[32,4,4096]{2,1,0:T(4,128)(2,1)} %stack.2), calls=%async_computation.4 | async-start | bytes 2097152 | tf_op jit(solution)/shard_map/all_to_all | solution.py:13
  393.2 30.3 %all-to-all-start.5 = ((bf16[128,32,128]{2,0,1:T(8,128)(2,1)}), bf16[128,32,128]{2,0,1:T(8,128)(2,1)}, u32[]{:S(2)}, u32[]{:S(2)}) async-start(bf16[128,32,128]{2,0,1:T(8,128)(2,1)} %fusion.42), calls=%async_computation.5 | async-start | bytes 2097152 | tf_op jit(solution)/shard_map/all_to_all | solution.py:222
  538.8 3.1 copy-start.1
  538.8 3.1 copy-start.13
  538.8 3.1 copy-start.17
  541.9 3.8 copy-start.4
  545.7 10.9 %copy-start.2 = (f32[4352,1,128]{2,0,1:T(8,128)S(1)}, f32[4352,1,128]{2,0,1:T(8,128)}, u32[]{:S(2)}) copy-start(f32[4352,1,128]{2,0,1:T(8,128)} %get-tuple-element.111) | copy-start | bytes 6684676
  548.9 29.8 %all-to-all-start.6 = ((bf16[32,128,128]{1,2,0:T(8,128)(2,1)}), bf16[32,128,128]{1,2,0:T(8,128)(2,1)S(1)}, u32[]{:S(2)}, u32[]{:S(2)}) async-start(bf16[32,128,128]{1,2,0:T(8,128)(2,1)} %multiply_convert_fusion), calls=%async_computation.6 | async-start | bytes 2097152 | tf_op jit(solution)/shard_map/all_to_all | solution.py:225
  578.7 1.0 copy-start.7
  579.7 52.5 %all-to-all-start.7 = ((f32[32,128,128]{1,2,0:T(8,128)}), f32[32,128,128]{1,2,0:T(8,128)S(1)}, u32[]{:S(2)}, u32[]{:S(2)}) async-start(f32[32,128,128]{1,2,0:T(8,128)} %copy.117), calls=%async_computation.7 | async-start | bytes 4194304 | tf_op jit(solution)/shard_map/all_to_all | solution.py:233
  593.5 47.1 %copy-start.15 = (f32[128]{0:T(128)S(1)}, f32[128]{0:T(128)}, u32[]{:S(2)}) copy-start(f32[128]{0:T(128)} %param.17) | copy-start | bytes 1540
  632.2 54.1 %all-to-all-start.8 = ((f32[32,128,128]{1,2,0:T(8,128)}), f32[32,128,128]{1,2,0:T(8,128)}, u32[]{:S(2)}, u32[]{:S(2)}) async-start(f32[32,128,128]{1,2,0:T(8,128)} %copy.121), calls=%async_computation.8 | async-start | bytes 4194304 | tf_op jit(solution)/shard_map/all_to_all | solution.py:240
  640.6 2.5 copy-start.6
  640.6 2.5 copy-start.12
  644.8 44.3 %copy-start.20 = (f32[128]{0:T(128)S(1)}, f32[128]{0:T(128)}, u32[]{:S(2)}) copy-start(f32[128]{0:T(128)} %get-tuple-element.153) | copy-start | bytes 1540
Sparse Core Ops, SparseCore 0:
  195.8 162.1 all-reduce.9
